TPU v7x, 512 devices: a whole 4x4x16 slice. The times are simulated.
512 devices in a mesh: gx: 16 (over x, z_hi, core), gy: 32 (over z_lo, y).
Axes of the slice: x: 4, y: 4, z: 16 (z_hi: 2, z_lo: 8; z = z_hi * 8 + z_lo), core: 2. Of those that a mesh axis runs over, the one named last changes fastest.
Arguments:
- fine_multipoles: bfloat16 [32, 32, 32, 2, 256], P('gx', 'gy'), may hold values from -6 to 6
- m2m_ops: bfloat16 [2, 2, 2, 256, 256], replicated, may hold values from -0.125 to 0.125
- m2l_ops: bfloat16 [512, 256, 256], P('gy'), may hold values from -0.015625 to 0.015625
- offsets: int32 [512, 3], P('gy'), may hold values from -7 to 7, as said below
Outputs:
- local_expansions: float32 [16, 256, 2, 256], P('gx', 'gy')
Inputs may be any that keep to these rules, and one draw needn't show every extreme that they name: Rows are distinct offsets; the first component lies in -3 to 3; in each row the largest magnitude of the three components is 2 or more.
All inputs are finite; a program needn't handle non-finite values.
Results may differ from a plain program's by a relative error of at most 0.0029.
Values may be sent and summed in bfloat16 or wider, within the bound.
A program may use at most 64 MiB of HBM per device.

v0:
```python
import jax
import jax.numpy as jnp
from jax import lax
from jax.sharding import PartitionSpec as P


def from_partner(array, axis, stride):
    return lax.ppermute(array, axis, [(i, i ^ 1 << stride) for i in range(lax.axis_size(axis))])


def passed_along(value, axis, steps):
    count = lax.axis_size(axis)
    pairs = [(source, (source + steps) % count) for source in range(count)]
    return lax.ppermute(value, axis, pairs)


def on_device(fine_multipoles, m2m_ops, m2l_ops, offsets):
    fine_boxes = fine_multipoles.shape[2]
    charge_sets = fine_multipoles.shape[3]
    coeffs = fine_multipoles.shape[4]
    half_z = fine_boxes // 2
    quarter = half_z // 2
    y_index = lax.axis_index("gy")
    parity = y_index % 2
    selected = lax.dynamic_index_in_dim(m2m_ops, parity, 1, keepdims=False)
    children = fine_multipoles[:, 0].reshape(2, half_z, 2, charge_sets, coeffs)
    partial_value = jnp.einsum(
        "azcri,acio->zro", children, selected, preferred_element_type=jnp.float32
    )
    kept_half = lax.dynamic_slice_in_dim(partial_value, parity * quarter, quarter, 0)
    sent_half = lax.dynamic_slice_in_dim(partial_value, (1 - parity) * quarter, quarter, 0)
    arrived = from_partner(sent_half, "gy", 0)
    coarse_mine = (kept_half + arrived).astype(jnp.bfloat16)
    slab_boxes = lax.all_gather(coarse_mine, "gy", axis=0, tiled=True)
    ahead_planes = [passed_along(slab_boxes, "gx", -distance) for distance in (1, 2, 3)]
    behind_planes = [passed_along(slab_boxes, "gx", distance) for distance in (1, 2, 3)]
    stacked = jnp.stack(behind_planes[::-1] + [slab_boxes] + ahead_planes)
    coarse_rows = slab_boxes.shape[0] // half_z
    plane_grid = stacked.reshape(7, coarse_rows, half_z, charge_sets, coeffs)
    count_ops = m2l_ops.shape[0]
    sources = []
    for op_entry in range(count_ops):
        shift_row = offsets[op_entry]
        chosen_plane = lax.dynamic_index_in_dim(plane_grid, shift_row[0] + 3, 0, keepdims=False)
        rolled = jnp.roll(chosen_plane, (-shift_row[1], -shift_row[2]), axis=(0, 1))
        sources.append(rolled.reshape(coarse_rows * half_z, charge_sets, coeffs))
    summed = jnp.zeros((quarter * lax.axis_size("gy") * charge_sets, coeffs), jnp.float32)
    for op_entry in range(count_ops):
        row_block = sources[op_entry].reshape(quarter * lax.axis_size("gy") * charge_sets, coeffs)
        summed = summed + jnp.dot(row_block, m2l_ops[op_entry], preferred_element_type=jnp.float32)
    my_locals = lax.psum_scatter(
        summed.reshape(quarter * lax.axis_size("gy"), charge_sets, coeffs),
        "gy",
        scatter_dimension=0,
        tiled=True,
    )
    return my_locals[None]


def solution(mesh):
    return jax.shard_map(
        on_device,
        mesh=mesh,
        in_specs=(P("gx", "gy", None, None, None), P(), P("gy", None, None), P("gy", None)),
        out_specs=P("gx", "gy", None, None),
        check_vma=False,
    )
```

profile of v0, /device:TPU:2, one launch (start us, length us, event | category | flops | bytes accessed | tf_op | source)
XLA Modules:
  0.0 762.8 jit_solution(14882671886684901363)
XLA Ops:
  6.5 1.2 copy-done
  7.8 1.0 convolution_bitcast_fusion
  8.8 3.5 collective-permute-start
  12.3 2.1 collective-permute-done
  14.5 127.3 %all_gather.3 = bf16[256,2,256]{2,0,1:T(8,128)(2,1)S(1)} all-gather(bf16[8,2,256]{2,0,1:T(8,128)(2,1)S(1)} %fusion.71), channel_id=1, replica_groups=mesh['gx'=16,'gy'=32] {'gy'}, dimensions={0}, use_global_device_ids=true | all-gather | bytes 270336 | tf_op jit(solution)/shard_map/all_gather | solution.py:34
  141.8 1.9 collective-permute-start.1
  143.7 2.1 fusion.73
  148.5 2.1 fusion.74
  163.8 8.3 %collective-permute-start.2 = (bf16[256,2,256]{2,0,1:T(8,128)(2,1)S(1)}, bf16[256,2,256]{2,0,1:T(8,128)(2,1)S(1)}, u32[]{:S(2)}, u32[]{:S(2)}) collective-permute-start(bf16[256,2,256]{2,0,1:T(8,128)(2,1)S(1)} %all_gather.3), channel_id=1, source_target_pairs={{0,64},{32,96},{64,128},{96,160},{128,192},{160,224},{192,256},{22... | collective-permute-start | bytes 786440 | tf_op jit(solution)/shard_map/ppermute | solution.py:14
  172.1 1.7 fusion.75
  183.4 3.3 collective-permute-start.3
  201.7 11.9 %collective-permute-start.4 = (bf16[256,2,256]{2,0,1:T(8,128)(2,1)S(1)}, bf16[256,2,256]{2,0,1:T(8,128)(2,1)S(1)}, u32[]{:S(2)}, u32[]{:S(2)}) collective-permute-start(bf16[256,2,256]{2,0,1:T(8,128)(2,1)S(1)} %all_gather.3), channel_id=1, source_target_pairs={{0,480},{32,0},{64,32},{96,64},{128,96},{160,128},{192,160},{224,1... | collective-permute-start | bytes 786440 | tf_op jit(solution)/shard_map/ppermute | solution.py:14
  213.6 6.3 collective-permute-start.5
  219.9 2.1 collective-permute-start.6
  222.1 1.9 collective-permute-done.4
  224.0 7.5 collective-permute-done.5
  231.5 4.8 collective-permute-done.6
  236.3 1.5 constant_dynamic-slice_fusion
  237.8 1.2 copy_bitcast_fusion
  239.7 0.7 fusion.4
  240.4 0.8 reshape_reshape.62
  241.2 2.3 copy_bitcast_fusion.2
  244.1 0.7 fusion.6
  244.9 0.8 reshape_reshape.61
  245.7 1.6 fusion.9
  247.3 0.7 fusion.8
  248.0 0.8 reshape_reshape.60
  248.8 2.3 copy_bitcast_fusion.4
  251.8 0.7 fusion.10
  252.5 0.8 reshape_reshape.59
  253.3 1.6 fusion.13
  255.0 0.7 fusion.12
  255.7 0.8 reshape_reshape.58
  256.5 2.3 copy_bitcast_fusion.6
  259.4 1.0 fusion.14
  260.4 0.8 reshape_reshape.57
  261.2 1.6 fusion.17
  262.8 0.7 fusion.16
  263.6 0.8 reshape_reshape.56
  264.4 1.3 copy_bitcast_fusion.8
  266.3 0.7 fusion.18
  267.0 0.8 reshape_reshape.55
  267.8 1.6 fusion.21
  270.2 0.8 reshape_reshape.54
  272.2 0.7 fusion.22
  273.0 0.8 reshape_reshape.53
  275.2 0.8 reshape_reshape.52
  278.0 0.8 reshape_reshape.51
  278.8 0.9 fusion.29
  280.4 0.8 reshape_reshape.50
  281.2 1.3 copy_bitcast_fusion.14
  283.9 0.8 reshape_reshape.49
  284.7 1.6 fusion.33
  286.3 1.5 fusion.32
  287.8 1.1 reshape_reshape.48
  288.8 1.6 fusion.3
  290.5 1.5 fusion.2
  291.9 1.8 reshape_reshape.63
  293.9 1.2 convolution_add_fusion.14
  299.4 1.1 convolution_add_fusion
  300.5 1.1 reshape.242
  301.6 1.3 dynamic-slice.8
  303.5 451.1 %all-reduce.3.cloned.1.call-done = f32[256,2,256]{2,1,0:T(2,128)} async-done(((f32[256,2,256]{2,1,0:T(2,128)}), f32[256,2,256]{2,1,0:T(2,128)}) %all-reduce.3.cloned.1.call-update) | async-done | bytes 524304
  754.6 1.3 dynamic-slice_bitcast_fusion
  (75 shorter events, 15.2 us)
Async XLA Ops:
  6.5 1.2 copy-start
  6.5 748.1 %all-reduce.3.cloned.1.call-start = ((), (), s32[]{:S(2)}) async-start(), calls=%async_computation | async-start | bytes 1048576
  8.8 5.6 collective-permute-start
  141.8 78.1 %collective-permute-start.1 = (bf16[256,2,256]{2,0,1:T(8,128)(2,1)S(1)}, bf16[256,2,256]{2,0,1:T(8,128)(2,1)S(1)}, u32[]{:S(2)}, u32[]{:S(2)}) collective-permute-start(bf16[256,2,256]{2,0,1:T(8,128)(2,1)S(1)} %all_gather.3), channel_id=1, source_target_pairs={{0,96},{32,128},{64,160},{96,192},{128,224},{160,256},{192,288},{2... | collective-permute-start | bytes 786440 | tf_op jit(solution)/shard_map/ppermute | solution.py:14
  163.8 58.2 %collective-permute-start.2 = (bf16[256,2,256]{2,0,1:T(8,128)(2,1)S(1)}, bf16[256,2,256]{2,0,1:T(8,128)(2,1)S(1)}, u32[]{:S(2)}, u32[]{:S(2)}) collective-permute-start(bf16[256,2,256]{2,0,1:T(8,128)(2,1)S(1)} %all_gather.3), channel_id=1, source_target_pairs={{0,64},{32,96},{64,128},{96,160},{128,192},{160,224},{192,256},{22... | collective-permute-start | bytes 786440 | tf_op jit(solution)/shard_map/ppermute | solution.py:14
  183.4 38.7 %collective-permute-start.3 = (bf16[256,2,256]{2,0,1:T(8,128)(2,1)S(1)}, bf16[256,2,256]{2,0,1:T(8,128)(2,1)S(1)}, u32[]{:S(2)}, u32[]{:S(2)}) collective-permute-start(bf16[256,2,256]{2,0,1:T(8,128)(2,1)S(1)} %all_gather.3), channel_id=1, source_target_pairs={{0,32},{32,64},{64,96},{96,128},{128,160},{160,192},{192,224},{224... | collective-permute-start | bytes 786440 | tf_op jit(solution)/shard_map/ppermute | solution.py:14
  201.7 22.3 %collective-permute-start.4 = (bf16[256,2,256]{2,0,1:T(8,128)(2,1)S(1)}, bf16[256,2,256]{2,0,1:T(8,128)(2,1)S(1)}, u32[]{:S(2)}, u32[]{:S(2)}) collective-permute-start(bf16[256,2,256]{2,0,1:T(8,128)(2,1)S(1)} %all_gather.3), channel_id=1, source_target_pairs={{0,480},{32,0},{64,32},{96,64},{128,96},{160,128},{192,160},{224,1... | collective-permute-start | bytes 786440 | tf_op jit(solution)/shard_map/ppermute | solution.py:14
  213.6 17.9 %collective-permute-start.5 = (bf16[256,2,256]{2,0,1:T(8,128)(2,1)S(1)}, bf16[256,2,256]{2,0,1:T(8,128)(2,1)S(1)}, u32[]{:S(2)}, u32[]{:S(2)}) collective-permute-start(bf16[256,2,256]{2,0,1:T(8,128)(2,1)S(1)} %all_gather.3), channel_id=1, source_target_pairs={{0,448},{32,480},{64,0},{96,32},{128,64},{160,96},{192,128},{224,1... | collective-permute-start | bytes 786440 | tf_op jit(solution)/shard_map/ppermute | solution.py:14
  219.9 16.4 %collective-permute-start.6 = (bf16[256,2,256]{2,0,1:T(8,128)(2,1)S(1)}, bf16[256,2,256]{2,0,1:T(8,128)(2,1)S(1)}, u32[]{:S(2)}, u32[]{:S(2)}) collective-permute-start(bf16[256,2,256]{2,0,1:T(8,128)(2,1)S(1)} %all_gather.3), channel_id=1, source_target_pairs={{0,416},{32,448},{64,480},{96,0},{128,32},{160,64},{192,96},{224,1... | collective-permute-start | bytes 786440 | tf_op jit(solution)/shard_map/ppermute | solution.py:14
  283.2 10.5 %copy-start.1 = (bf16[16,256,256]{2,1,0:T(8,128)(2,1)S(1)}, bf16[16,256,256]{2,1,0:T(8,128)(2,1)}, u32[]{:S(2)}) copy-start(bf16[16,256,256]{2,1,0:T(8,128)(2,1)} %param.8) | copy-start | bytes 6291460
  293.7 1.5 copy-start.15
  293.7 1.7 copy-start.13
  293.9 1.8 copy-start.12
  295.2 1.0 copy-start.11
  295.4 1.0 copy-start.10
  295.7 1.0 copy-start.9
  296.1 1.0 copy-start.8
  296.4 1.0 copy-start.7
  296.7 1.0 copy-start.6
  297.1 1.0 copy-start.5
  297.4 1.0 copy-start.4
  297.7 1.0 copy-start.3
  298.1 1.0 copy-start.2
  298.4 1.0 copy-start.14
Sparse Core Ops, SparseCore 0:
  301.7 452.8 all-reduce.2
where the time goes:
time: 764 us; the launch traced here: 763 us
  waiting for transfers between devices  467 us (61%)
  blocking collectives  127 us (17%)
  between operations  55 us (7%)
  local copies, waits for them, and re-layouts  39.3 us (5%)
  starting transfers between devices  37.2 us (5%)
  other arithmetic  30.1 us (4%)
    unnamed x2, waiting for transfers between devices  451 us
    all_gather x1, blocking collectives, on_device(): slab_boxes = lax.all_gather(coarse_mine, 'gy', axis=0, tiled=True)  127 us
    ppermute x6, starting transfers between devices, passed_along(): return lax.ppermute(value, axis, pairs)  33.7 us
    concatenate x32, other arithmetic, on_device(): rolled = jnp.roll(chosen_plane, (-shift_row[1], -shift_row[2]), axis=(0, 1))  30 us
  transfers between devices with their start and end apart: 8, of which 5 were waited for; matrix products, arithmetic and copies ran while one was open for 1% of the time, Pallas kernels for 0%

commit v1 on v0

v1 whole, which is shorter than its diff:
```python
import functools

import jax
import jax.numpy as jnp
from jax import lax
from jax.experimental import pallas as pl
from jax.experimental.pallas import tpu as pltpu
from jax.sharding import PartitionSpec as P

MESH = pl.DeviceIdType.MESH
VMEM = pl.BlockSpec(memory_space=pltpu.VMEM)
SMEM = pl.BlockSpec(memory_space=pltpu.SMEM)


def place():
    gx, gy = lax.axis_index("gx"), lax.axis_index("gy")
    return gx // 4, gx // 2 % 2, gx % 2, gy // 4, gy % 4


def device(x, zh, core, zl, y):
    return (x * 4 + zh * 2 + core, zl * 4 + y)


def greet(peers):
    barrier = pltpu.get_barrier_semaphore()
    for peer in peers:
        pl.semaphore_signal(barrier, inc=1, device_id=peer, device_id_type=MESH)
    pl.semaphore_wait(barrier, len(peers))


def first_shared(zh_block, zh, sender_core):
    return jnp.where(zh_block < zh, 1, jnp.where(zh_block > zh, 0, 1 - sender_core))


def gather_kernel(mine, held, other, local_sem, x_send, x_recv, y_send, y_recv, r_send, r_recv, l_send, l_recv, c_send, c_recv):
    x, zh, core, zl, y = place()
    zp = zh * 8 + zl
    after = (zp + 1) % 16
    before = (zp + 15) % 16
    x_next = device((x + 1) % 4, zh, core, zl, y)
    x_last = device((x + 3) % 4, zh, core, zl, y)
    y_peers = [device(x, zh, core, zl, (y + d) % 4) for d in (1, 2, 3)]
    z_next = device(x, after // 8, core, after % 8, y)
    z_last = device(x, before // 8, core, before % 8, y)
    partner = device(x, zh, 1 - core, zl, y)

    def remote(src, dst, send, recv, target):
        return pltpu.make_async_remote_copy(
            src_ref=src, dst_ref=dst, send_sem=send, recv_sem=recv, device_id=target, device_id_type=MESH
        )

    own = pltpu.make_async_copy(mine, held.at[zp, 1, y], local_sem)
    own.start()
    greet([x_next, x_last, *y_peers, z_next, z_last, partner])
    along_x = [
        remote(mine, held.at[zp, 0, y], x_send.at[0], x_recv.at[0], x_next),
        remote(mine, held.at[zp, 2, y], x_send.at[1], x_recv.at[1], x_last),
    ]
    for copy in along_x:
        copy.start()
    own.wait()
    for copy in along_x:
        copy.wait()
    along_y = [
        remote(held.at[zp, :, y], held.at[zp, :, y], y_send.at[d], y_recv.at[d], y_peers[d]) for d in range(3)
    ]
    for copy in along_y:
        copy.start()
    for copy in along_y:
        copy.wait()

    def right(step, slot):
        block = held.at[(zp + 16 - step) % 16, slot]
        return remote(block, block, r_send.at[step, slot], r_recv.at[step, slot], z_next)

    def left(step, slot):
        block = held.at[(zp + step) % 16, slot]
        return remote(block, block, l_send.at[step, slot], l_recv.at[step, slot], z_last)

    def share(position):
        start = first_shared(position // 8, zh, core)
        return remote(held.at[position, pl.ds(start, 2)], other.at[position], c_send.at[position], c_recv.at[position], partner)

    for slot in range(3):
        right(0, slot).start()
        left(0, slot).start()
    share(zp).start()

    def advance(step, carry):
        for slot in range(3):
            right(step - 1, slot).wait_recv()
            right(step, slot).start()
            left(step - 1, slot).wait_recv()

            @pl.when(step < 7)
            def _():
                left(step, slot).start()

        share((zp + 16 - step) % 16).start()
        share((zp + step) % 16).start()
        return carry

    lax.fori_loop(1, 8, advance, 0)
    for slot in range(3):
        right(7, slot).wait_recv()
    share((zp + 8) % 16).start()

    def drain(step, carry):
        for slot in range(3):
            right(step, slot).wait_send()

            @pl.when(step < 7)
            def _():
                left(step, slot).wait_send()

        share(step).wait()
        share(step + 8).wait()
        return carry

    lax.fori_loop(0, 8, drain, 0)


def gather_planes(mine):
    dma = pltpu.SemaphoreType.DMA
    return pl.pallas_call(
        gather_kernel,
        out_shape=[
            jax.ShapeDtypeStruct((16, 3, 4, 16, 256), jnp.bfloat16),
            jax.ShapeDtypeStruct((16, 2, 4, 16, 256), jnp.bfloat16),
        ],
        in_specs=[VMEM],
        out_specs=[VMEM, VMEM],
        scratch_shapes=[
            dma,
            dma((2,)), dma((2,)),
            dma((3,)), dma((3,)),
            dma((8, 3)), dma((8, 3)),
            dma((7, 3)), dma((7, 3)),
            dma((16,)), dma((16,)),
        ],
        compiler_params=pltpu.CompilerParams(collective_id=0, has_side_effects=True),
        name="gather_planes",
    )(mine)


def translate_kernel(spot, offsets, held, other, ops, out, planes, total):
    zh, core = spot[0], spot[1]
    for shift in range(-3, 4):
        reach = shift + zh * 2 + core + 4
        slot = reach // 4
        zh_from = reach % 4 // 2
        if shift % 2:
            slot = slot - first_shared(zh_from, zh, 1 - core)
        source = other if shift % 2 else held
        for zl in range(8):
            rows = source[zh_from * 8 + zl, slot].astype(jnp.float32)
            for half in range(2):
                line = rows[half * 32 : half * 32 + 32]
                for part in range(2):
                    piece = line[:, part * 128 : part * 128 + 128]
                    planes[part, shift + 3, zl * 2 + half, 0:32] = piece
                    planes[part, shift + 3, zl * 2 + half, 32:64] = piece
    total[...] = jnp.zeros_like(total)

    def one(entry, carry):
        dx, dy, dz = offsets[entry, 0] + 3, offsets[entry, 1], offsets[entry, 2]
        start = 2 * ((dz + 16) & 15)
        halves = [
            jnp.concatenate([planes[part, dx, (line + dy + 16) & 15, pl.ds(start, 32), :] for line in range(16)], axis=0)
            for part in range(2)
        ]
        rolled = jnp.concatenate(halves, axis=1).astype(jnp.bfloat16)
        total[...] += jnp.dot(rolled, ops[entry], preferred_element_type=jnp.float32)
        return carry

    lax.fori_loop(0, 16, one, 0)
    out[...] = total[...].astype(jnp.bfloat16)


def translate(spot, offsets, held, other, ops):
    return pl.pallas_call(
        translate_kernel,
        out_shape=jax.ShapeDtypeStruct((512, 256), jnp.bfloat16),
        in_specs=[SMEM, SMEM, VMEM, VMEM, VMEM],
        out_specs=VMEM,
        scratch_shapes=[pltpu.VMEM((2, 7, 16, 64, 128), jnp.float32), pltpu.VMEM((512, 256), jnp.float32)],
        name="translate",
    )(spot, offsets, held, other, ops)


def scatter_kernel(part, out, from_y, summed, rounded, from_z, y_send, y_recv, z_send, z_recv):
    x, zh, core, zl, y = place()
    y_of = [(y + d) % 4 for d in (1, 2, 3)]
    z_of = [(zl + d) % 8 for d in range(1, 8)]
    y_peers = [device(x, zh, core, zl, to) for to in y_of]
    z_peers = [device(x, zh, core, to, y) for to in z_of]
    greet(y_peers + z_peers)
    along_y = [
        pltpu.make_async_remote_copy(
            src_ref=part.at[:, y_of[d]], dst_ref=from_y.at[d], send_sem=y_send.at[d], recv_sem=y_recv.at[d],
            device_id=y_peers[d], device_id_type=MESH,
        )
        for d in range(3)
    ]
    for copy in along_y:
        copy.start()
    for copy in along_y:
        copy.wait()
    row = part[:, y].astype(jnp.float32)
    for d in range(3):
        row = row + from_y[d].astype(jnp.float32)
    summed[...] = row
    rounded[...] = row.astype(jnp.bfloat16)
    along_z = [
        pltpu.make_async_remote_copy(
            src_ref=rounded.at[z_of[d]], dst_ref=from_z.at[d], send_sem=z_send.at[d], recv_sem=z_recv.at[d],
            device_id=z_peers[d], device_id_type=MESH,
        )
        for d in range(7)
    ]
    for copy in along_z:
        copy.start()
    for copy in along_z:
        copy.wait()
    result = summed[zl]
    for d in range(7):
        result = result + from_z[d].astype(jnp.float32)
    out[...] = result


def scatter_sums(part):
    dma = pltpu.SemaphoreType.DMA
    return pl.pallas_call(
        scatter_kernel,
        out_shape=jax.ShapeDtypeStruct((16, 256), jnp.float32),
        in_specs=[VMEM],
        out_specs=VMEM,
        scratch_shapes=[
            pltpu.VMEM((3, 8, 16, 256), jnp.bfloat16),
            pltpu.VMEM((8, 16, 256), jnp.float32),
            pltpu.VMEM((8, 16, 256), jnp.bfloat16),
            pltpu.VMEM((7, 16, 256), jnp.bfloat16),
            dma((3,)), dma((3,)), dma((7,)), dma((7,)),
        ],
        compiler_params=pltpu.CompilerParams(collective_id=1, has_side_effects=True),
        name="scatter_sums",
    )(part)


def on_device(fine_multipoles, m2m_ops, m2l_ops, offsets):
    parity = lax.axis_index("gy") % 2
    selected = lax.dynamic_index_in_dim(m2m_ops, parity, 1, keepdims=False)
    children = fine_multipoles[:, 0].reshape(2, 16, 2, 2, 256)
    partial = jnp.einsum("azcri,acio->zro", children, selected, preferred_element_type=jnp.float32)
    kept = lax.dynamic_slice_in_dim(partial, parity * 8, 8, 0)
    sent = lax.dynamic_slice_in_dim(partial, (1 - parity) * 8, 8, 0)
    arrived = lax.ppermute(sent, "gy", [(i, i ^ 1) for i in range(32)])
    mine = (kept + arrived).astype(jnp.bfloat16).reshape(16, 256)
    held, other = gather_planes(mine)
    gx = lax.axis_index("gx")
    spot = jnp.stack([gx // 2 % 2, gx % 2]).astype(jnp.int32)
    part = translate(spot, offsets, held.reshape(16, 3, 64, 256), other.reshape(16, 2, 64, 256), m2l_ops)
    result = scatter_sums(part.reshape(8, 4, 16, 256))
    return result.reshape(1, 8, 2, 256)


def solution(mesh):
    return jax.shard_map(
        on_device,
        mesh=mesh,
        in_specs=(P("gx", "gy", None, None, None), P(), P("gy", None, None), P("gy", None)),
        out_specs=P("gx", "gy", None, None),
        check_vma=False,
    )
```

time: 764 us -> 88.1 us (0.12)
  the two profiles are of different devices: /device:TPU:2 before, /device:TPU:1 now
where the time goes in v1:
time: 88.1 us; the launch traced here: 87.7 us
  Pallas kernels  77.4 us (88%)
  local copies, waits for them, and re-layouts  4.54 us (5%)
  starting transfers between devices  4.02 us (5%)
  matrix products  1.03 us (1%)
    pallas_call x1, Pallas kernels, gather_planes(): pl.pallas_call(gather_kernel, out_shape=[jax.ShapeDtypeStruct((16, 3, 4,...  53.3 us
    pallas_call x1, Pallas kernels, scatter_sums(): pl.pallas_call(scatter_kernel, out_shape=jax.ShapeDtypeStruct((16, 256),...  16.7 us
    pallas_call x1, Pallas kernels, translate(): pl.pallas_call(translate_kernel, out_shape=jax.ShapeDtypeStruct((512, 256...  7.41 us
    ppermute x1, starting transfers between devices, on_device(): arrived = lax.ppermute(sent, 'gy', [(i, i ^ 1) for i in range(32)])  4.02 us
    unnamed x3, local copies, waits for them, and re-layouts  2.58 us
  transfers between devices with their start and end apart: 1, of which 0 were waited for; matrix products, arithmetic and copies ran while one was open for 2% of the time, Pallas kernels for 0%

profile of v1, /device:TPU:1, one launch (start us, length us, event | category | flops | bytes accessed | tf_op | source)
XLA Modules:
  0.0 87.7 jit_solution(7912995303761000494)
XLA Ops:
  0.0 0.0 copy-start
  0.0 1.2 %copy-done = bf16[2,2,2,256,256]{4,3,2,1,0:T(8,128)(2,1)S(1)} copy-done((bf16[2,2,2,256,256]{4,3,2,1,0:T(8,128)(2,1)S(1)}, bf16[2,2,2,256,256]{4,3,2,1,0:T(8,128)(2,1)}, u32[]{:S(2)}) %copy-start) | copy-done | bytes 1048600
  1.2 1.0 %convolution_bitcast_fusion = f32[256,16,2]{0,1,2:T(8,128)S(1)} fusion(bf16[2,2,2,256,256]{4,3,2,1,0:T(8,128)(2,1)S(1)} %copy-done, s32[]{:T(128)S(6)} %select_n.33, bf16[2,16,2,2,256]{4,3,2,1,0:T(2,128)(2,1)} %bitcast.25), kind=kOutput, calls=%fused_computation | convolution fusion | flops 16777216 | bytes 622596 | tf_op jit(solution)/shard_map/azcri,acio->zro/dot_general | solution.py:254
  2.3 4.0 %collective-permute-start = (f32[8,2,256]{2,0,1:T(8,128)S(1)}, f32[8,2,256]{2,0,1:T(8,128)S(1)}, u32[]{:S(2)}, u32[]{:S(2)}) collective-permute-start(f32[8,2,256]{2,0,1:T(8,128)S(1)} %dynamic-slice_bitcast_fusion), channel_id=1, source_target_pairs={{0,1},{1,0},{2,3},{3,2},{4,5},{5,4},{6,7},{7,6},{8,9},{9,8},{10,11... | collective-permute-start | bytes 49160 | tf_op jit(solution)/shard_map/ppermute | solution.py:257
  6.3 0.6 pad_add_fusion.spot
  7.0 1.4 %copy.7.offsets = s32[16,3]{1,0:T(8,128)} copy(s32[16,3]{0,1:T(4,128)} %param.7) | data formatting | bytes 384 | tf_op args[3]
  8.3 0.0 collective-permute-done
  8.3 0.6 reshape.15.mine
  8.9 53.3 %gather_planes.1 = (bf16[16,3,4,16,256]{4,3,2,1,0:T(8,128)(2,1)}, bf16[16,2,4,16,256]{4,3,2,1,0:T(8,128)(2,1)}) custom-call(bf16[16,256]{1,0:T(8,128)(2,1)} %reshape.15.mine), custom_call_target="tpu_custom_call" | custom-call | tf_op jit(solution)/shard_map/gather_planes/pallas_call | solution.py:125
  62.2 7.4 %translate.1 = bf16[512,256]{1,0:T(8,128)(2,1)} custom-call(s32[2]{0:T(128)} %pad_add_fusion.spot, s32[16,3]{1,0:T(8,128)} %copy.7.offsets, bf16[16,3,64,256]{3,2,1,0:T(8,128)(2,1)} %bitcast.22, bf16[16,2,64,256]{3,2,1,0:T(8,128)(2,1)} %bitcast.23, bf16[16,256,256]{2,1,0:T(8,128)(2,1)} %ops.1), custom_call_target="tpu_custom_call" | custom-call | tf_op jit(solution)/shard_map/translate/pallas_call | solution.py:181
  69.6 16.7 %scatter_sums.1 = f32[16,256]{1,0:T(8,128)} custom-call(bf16[8,4,16,256]{3,2,1,0:T(8,128)(2,1)} %bitcast.24), custom_call_target="tpu_custom_call" | custom-call | tf_op jit(solution)/shard_map/scatter_sums/pallas_call | solution.py:233
  86.4 1.3 %reshape.19 = f32[1,8,2,256]{3,2,1,0:T(2,128)} reshape(f32[16,256]{1,0:T(8,128)} %scatter_sums.1) | data formatting | bytes 32768 | tf_op jit(solution)/shard_map/reshape | solution.py:264
  (3 shorter events, 0.0 us)
Async XLA Ops:
  0.0 1.2 %copy-start = (bf16[2,2,2,256,256]{4,3,2,1,0:T(8,128)(2,1)S(1)}, bf16[2,2,2,256,256]{4,3,2,1,0:T(8,128)(2,1)}, u32[]{:S(2)}) copy-start(bf16[2,2,2,256,256]{4,3,2,1,0:T(8,128)(2,1)} %param.5) | copy-start | bytes 3145732
  2.3 6.0 %collective-permute-start = (f32[8,2,256]{2,0,1:T(8,128)S(1)}, f32[8,2,256]{2,0,1:T(8,128)S(1)}, u32[]{:S(2)}, u32[]{:S(2)}) collective-permute-start(f32[8,2,256]{2,0,1:T(8,128)S(1)} %dynamic-slice_bitcast_fusion), channel_id=1, source_target_pairs={{0,1},{1,0},{2,3},{3,2},{4,5},{5,4},{6,7},{7,6},{8,9},{9,8},{10,11... | collective-permute-start | bytes 49160 | tf_op jit(solution)/shard_map/ppermute | solution.py:257

commit v2 on v1

--- a/solution.py
+++ b/solution.py
@@ -28,115 +28,121 @@
     pl.semaphore_wait(barrier, len(peers))
 
 
-def first_shared(zh_block, zh, sender_core):
-    return jnp.where(zh_block < zh, 1, jnp.where(zh_block > zh, 0, 1 - sender_core))
-
-
-def gather_kernel(mine, held, other, local_sem, x_send, x_recv, y_send, y_recv, r_send, r_recv, l_send, l_recv, c_send, c_recv):
+def source_offset(turn):
+    return jnp.where(turn % 2 == 1, (turn + 1) // 2, (16 - turn // 2) % 16)
+
+
+LAG = 4
+
+
+def gather_kernel(mine, held, other, local_sem, z_send, z_recv, y_send, y_recv, x_send, x_recv, c_send, c_recv):
     x, zh, core, zl, y = place()
     zp = zh * 8 + zl
-    after = (zp + 1) % 16
-    before = (zp + 15) % 16
-    x_next = device((x + 1) % 4, zh, core, zl, y)
-    x_last = device((x + 3) % 4, zh, core, zl, y)
+    x_peers = [device((x + d) % 4, zh, core, zl, y) for d in (1, 3)]
     y_peers = [device(x, zh, core, zl, (y + d) % 4) for d in (1, 2, 3)]
-    z_next = device(x, after // 8, core, after % 8, y)
-    z_last = device(x, before // 8, core, before % 8, y)
     partner = device(x, zh, 1 - core, zl, y)
+
+    def z_peer(offset):
+        position = (zp + offset) % 16
+        return device(x, position // 8, core, position % 8, y)
 
     def remote(src, dst, send, recv, target):
         return pltpu.make_async_remote_copy(
             src_ref=src, dst_ref=dst, send_sem=send, recv_sem=recv, device_id=target, device_id_type=MESH
         )
 
-    own = pltpu.make_async_copy(mine, held.at[zp, 1, y], local_sem)
+    def along_z(offset):
+        to = (zp + offset) % 16
+        return remote(mine, held.at[1 + core + zh - to // 8, zl, y], z_send.at[offset], z_recv.at[offset], z_peer(offset))
+
+    def spot_of(turn):
+        position = (zp + 16 - source_offset(turn)) % 16
+        return position, 1 + core + position // 8 - zh, position % 8
+
+    def along_y(turn, d):
+        position, plane, row = spot_of(turn)
+        piece = held.at[plane, row, y]
+        return remote(piece, piece, y_send.at[position, d], y_recv.at[position, d], y_peers[d])
+
+    def along_x(turn):
+        position, plane, row = spot_of(turn)
+        to = (x + jnp.where(plane >= 2, 1, 3)) % 4
+        return remote(
+            held.at[plane, row], held.at[(plane + 2) % 4, row], x_send.at[position], x_recv.at[position],
+            device(to, zh, core, zl, y),
+        )
+
+    def across(turn, far):
+        position, plane, row = spot_of(turn)
+        plane = (plane + 2 * far) % 4
+        return remote(held.at[plane, row], other.at[plane, row], c_send.at[position, far], c_recv.at[position, far], partner)
+
+    own = pltpu.make_async_copy(mine, held.at[1 + core, zl, y], local_sem)
     own.start()
-    greet([x_next, x_last, *y_peers, z_next, z_last, partner])
-    along_x = [
-        remote(mine, held.at[zp, 0, y], x_send.at[0], x_recv.at[0], x_next),
-        remote(mine, held.at[zp, 2, y], x_send.at[1], x_recv.at[1], x_last),
-    ]
-    for copy in along_x:
-        copy.start()
+    greet([z_peer(d) for d in range(1, 16)] + y_peers + x_peers + [partner])
+
+    def send_z(turn, carry):
+        along_z((16 - source_offset(turn)) % 16).start()
+        return carry
+
+    lax.fori_loop(1, 16, send_z, 0)
     own.wait()
-    for copy in along_x:
-        copy.wait()
-    along_y = [
-        remote(held.at[zp, :, y], held.at[zp, :, y], y_send.at[d], y_recv.at[d], y_peers[d]) for d in range(3)
-    ]
-    for copy in along_y:
-        copy.start()
-    for copy in along_y:
-        copy.wait()
-
-    def right(step, slot):
-        block = held.at[(zp + 16 - step) % 16, slot]
-        return remote(block, block, r_send.at[step, slot], r_recv.at[step, slot], z_next)
-
-    def left(step, slot):
-        block = held.at[(zp + step) % 16, slot]
-        return remote(block, block, l_send.at[step, slot], l_recv.at[step, slot], z_last)
-
-    def share(position):
-        start = first_shared(position // 8, zh, core)
-        return remote(held.at[position, pl.ds(start, 2)], other.at[position], c_send.at[position], c_recv.at[position], partner)
-
-    for slot in range(3):
-        right(0, slot).start()
-        left(0, slot).start()
-    share(zp).start()
-
-    def advance(step, carry):
-        for slot in range(3):
-            right(step - 1, slot).wait_recv()
-            right(step, slot).start()
-            left(step - 1, slot).wait_recv()
-
-            @pl.when(step < 7)
+
+    def turns(turn, carry):
+        @pl.when(turn < 16)
+        def _():
+            @pl.when(turn > 0)
             def _():
-                left(step, slot).start()
-
-        share((zp + 16 - step) % 16).start()
-        share((zp + step) % 16).start()
-        return carry
-
-    lax.fori_loop(1, 8, advance, 0)
-    for slot in range(3):
-        right(7, slot).wait_recv()
-    share((zp + 8) % 16).start()
-
-    def drain(step, carry):
-        for slot in range(3):
-            right(step, slot).wait_send()
-
-            @pl.when(step < 7)
-            def _():
-                left(step, slot).wait_send()
-
-        share(step).wait()
-        share(step + 8).wait()
-        return carry
-
-    lax.fori_loop(0, 8, drain, 0)
+                along_z(source_offset(turn)).wait_recv()
+
+            for d in range(3):
+                along_y(turn, d).start()
+
+        @pl.when((turn >= LAG) & (turn < 16 + LAG))
+        def _():
+            for d in range(3):
+                along_y(turn - LAG, d).wait_recv()
+            along_x(turn - LAG).start()
+            across(turn - LAG, 0).start()
+
+        @pl.when(turn >= 2 * LAG)
+        def _():
+            along_x(turn - 2 * LAG).wait_recv()
+            across(turn - 2 * LAG, 1).start()
+
+        return carry
+
+    lax.fori_loop(0, 16 + 2 * LAG, turns, 0)
+
+    def drain(turn, carry):
+        @pl.when(turn > 0)
+        def _():
+            along_z(turn).wait_send()
+
+        for d in range(3):
+            along_y(turn, d).wait_send()
+        along_x(turn).wait_send()
+        across(turn, 0).wait()
+        across(turn, 1).wait()
+        return carry
+
+    lax.fori_loop(0, 16, drain, 0)
 
 
 def gather_planes(mine):
     dma = pltpu.SemaphoreType.DMA
+    planes = jax.ShapeDtypeStruct((4, 8, 4, 16, 256), jnp.bfloat16)
     return pl.pallas_call(
         gather_kernel,
-        out_shape=[
-            jax.ShapeDtypeStruct((16, 3, 4, 16, 256), jnp.bfloat16),
-            jax.ShapeDtypeStruct((16, 2, 4, 16, 256), jnp.bfloat16),
-        ],
+        out_shape=[planes, planes],
         in_specs=[VMEM],
         out_specs=[VMEM, VMEM],
         scratch_shapes=[
             dma,
-            dma((2,)), dma((2,)),
-            dma((3,)), dma((3,)),
-            dma((8, 3)), dma((8, 3)),
-            dma((7, 3)), dma((7, 3)),
             dma((16,)), dma((16,)),
+            dma((16, 3)), dma((16, 3)),
+            dma((16,)), dma((16,)),
+            dma((16, 2)), dma((16, 2)),
         ],
         compiler_params=pltpu.CompilerParams(collective_id=0, has_side_effects=True),
         name="gather_planes",
@@ -144,22 +150,17 @@
 
 
 def translate_kernel(spot, offsets, held, other, ops, out, planes, total):
-    zh, core = spot[0], spot[1]
     for shift in range(-3, 4):
-        reach = shift + zh * 2 + core + 4
-        slot = reach // 4
-        zh_from = reach % 4 // 2
-        if shift % 2:
-            slot = slot - first_shared(zh_from, zh, 1 - core)
-        source = other if shift % 2 else held
-        for zl in range(8):
-            rows = source[zh_from * 8 + zl, slot].astype(jnp.float32)
-            for half in range(2):
-                line = rows[half * 32 : half * 32 + 32]
-                for part in range(2):
-                    piece = line[:, part * 128 : part * 128 + 128]
-                    planes[part, shift + 3, zl * 2 + half, 0:32] = piece
-                    planes[part, shift + 3, zl * 2 + half, 32:64] = piece
+        for line in range(16):
+            rows = pl.ds(line * 32, 32)
+            if shift % 2:
+                wide = other[(shift + 3) // 2, rows].astype(jnp.float32)
+            else:
+                wide = held[(shift + 2) // 2 + spot[0], rows].astype(jnp.float32)
+            for part in range(2):
+                piece = wide[:, part * 128 : part * 128 + 128]
+                planes[part, shift + 3, line, 0:32] = piece
+                planes[part, shift + 3, line, 32:64] = piece
     total[...] = jnp.zeros_like(total)
 
     def one(entry, carry):
@@ -258,8 +259,8 @@
     mine = (kept + arrived).astype(jnp.bfloat16).reshape(16, 256)
     held, other = gather_planes(mine)
     gx = lax.axis_index("gx")
-    spot = jnp.stack([gx // 2 % 2, gx % 2]).astype(jnp.int32)
-    part = translate(spot, offsets, held.reshape(16, 3, 64, 256), other.reshape(16, 2, 64, 256), m2l_ops)
+    spot = (gx % 2).astype(jnp.int32).reshape(1)
+    part = translate(spot, offsets, held.reshape(4, 512, 256), other.reshape(4, 512, 256), m2l_ops)
     result = scatter_sums(part.reshape(8, 4, 16, 256))
     return result.reshape(1, 8, 2, 256)
 

time: 88.1 us -> 77.5 us (0.88)
  Pallas kernels: 77.4 us -> 67.5 us
    pallas_call x1, Pallas kernels: 53.3 us -> 43.2 us  [gather_planes(): pl.pallas_call(gather_kernel, out_shape=[planes, planes], in_specs=[VMEM]...]
where the time goes in v2:
time: 77.5 us; the launch traced here: 77.1 us
  Pallas kernels  67.5 us (87%)
  local copies, waits for them, and re-layouts  4.54 us (6%)
  starting transfers between devices  4.02 us (5%)
  matrix products  1.03 us (1%)
    pallas_call x1, Pallas kernels, gather_planes(): pl.pallas_call(gather_kernel, out_shape=[planes, planes], in_specs=[VMEM]...  43.2 us
    pallas_call x1, Pallas kernels, scatter_sums(): pl.pallas_call(scatter_kernel, out_shape=jax.ShapeDtypeStruct((16, 256),...  17 us
    pallas_call x1, Pallas kernels, translate(): pl.pallas_call(translate_kernel, out_shape=jax.ShapeDtypeStruct((512, 256...  7.23 us
    ppermute x1, starting transfers between devices, on_device(): arrived = lax.ppermute(sent, 'gy', [(i, i ^ 1) for i in range(32)])  4.02 us
    unnamed x3, local copies, waits for them, and re-layouts  2.58 us
  transfers between devices with their start and end apart: 1, of which 0 were waited for; matrix products, arithmetic and copies ran while one was open for 2% of the time, Pallas kernels for 0%

profile of v2, /device:TPU:1, one launch (start us, length us, event | category | flops | bytes accessed | tf_op | source)
XLA Modules:
  0.0 77.1 jit_solution(4391557859249274851)
XLA Ops:
  0.0 0.0 copy-start
  0.0 1.2 %copy-done = bf16[2,2,2,256,256]{4,3,2,1,0:T(8,128)(2,1)S(1)} copy-done((bf16[2,2,2,256,256]{4,3,2,1,0:T(8,128)(2,1)S(1)}, bf16[2,2,2,256,256]{4,3,2,1,0:T(8,128)(2,1)}, u32[]{:S(2)}) %copy-start) | copy-done | bytes 1048600
  1.2 1.0 %convolution_bitcast_fusion = f32[256,16,2]{0,1,2:T(8,128)S(1)} fusion(bf16[2,2,2,256,256]{4,3,2,1,0:T(8,128)(2,1)S(1)} %copy-done, s32[]{:T(128)S(6)} %select_n.23, bf16[2,16,2,2,256]{4,3,2,1,0:T(2,128)(2,1)} %bitcast.24), kind=kOutput, calls=%fused_computation | convolution fusion | flops 16777216 | bytes 622596 | tf_op jit(solution)/shard_map/azcri,acio->zro/dot_general | solution.py:255
  2.3 4.0 %collective-permute-start = (f32[8,2,256]{2,0,1:T(8,128)S(1)}, f32[8,2,256]{2,0,1:T(8,128)S(1)}, u32[]{:S(2)}, u32[]{:S(2)}) collective-permute-start(f32[8,2,256]{2,0,1:T(8,128)S(1)} %dynamic-slice_bitcast_fusion), channel_id=1, source_target_pairs={{0,1},{1,0},{2,3},{3,2},{4,5},{5,4},{6,7},{7,6},{8,9},{9,8},{10,11... | collective-permute-start | bytes 49160 | tf_op jit(solution)/shard_map/ppermute | solution.py:258
  6.3 1.4 %copy.7.offsets = s32[16,3]{1,0:T(8,128)} copy(s32[16,3]{0,1:T(4,128)} %param.7) | data formatting | bytes 384 | tf_op args[3]
  7.7 0.0 collective-permute-done
  7.7 0.6 reshape.19.mine
  8.3 43.2 %gather_planes.1 = (bf16[4,8,4,16,256]{4,3,2,1,0:T(8,128)(2,1)}, bf16[4,8,4,16,256]{4,3,2,1,0:T(8,128)(2,1)}) custom-call(bf16[16,256]{1,0:T(8,128)(2,1)} %reshape.19.mine), custom_call_target="tpu_custom_call" | custom-call | tf_op jit(solution)/shard_map/gather_planes/pallas_call | solution.py:135
  51.6 7.2 %translate.1 = bf16[512,256]{1,0:T(8,128)(2,1)} custom-call(s32[1]{0:T(128)} %bitcast.spot, s32[16,3]{1,0:T(8,128)} %copy.7.offsets, bf16[4,512,256]{2,1,0:T(8,128)(2,1)} %bitcast.21, bf16[4,512,256]{2,1,0:T(8,128)(2,1)} %bitcast.22, bf16[16,256,256]{2,1,0:T(8,128)(2,1)} %ops.1), custom_call_target="tpu_custom_call" | custom-call | tf_op jit(solution)/shard_map/translate/pallas_call | solution.py:182
  58.8 17.0 %scatter_sums.1 = f32[16,256]{1,0:T(8,128)} custom-call(bf16[8,4,16,256]{3,2,1,0:T(8,128)(2,1)} %bitcast.23), custom_call_target="tpu_custom_call" | custom-call | tf_op jit(solution)/shard_map/scatter_sums/pallas_call | solution.py:234
  75.8 1.3 %reshape.23 = f32[1,8,2,256]{3,2,1,0:T(2,128)} reshape(f32[16,256]{1,0:T(8,128)} %scatter_sums.1) | data formatting | bytes 32768 | tf_op jit(solution)/shard_map/reshape | solution.py:265
  (3 shorter events, 0.0 us)
Async XLA Ops:
  0.0 1.2 %copy-start = (bf16[2,2,2,256,256]{4,3,2,1,0:T(8,128)(2,1)S(1)}, bf16[2,2,2,256,256]{4,3,2,1,0:T(8,128)(2,1)}, u32[]{:S(2)}) copy-start(bf16[2,2,2,256,256]{4,3,2,1,0:T(8,128)(2,1)} %param.5) | copy-start | bytes 3145732
  2.3 5.4 %collective-permute-start = (f32[8,2,256]{2,0,1:T(8,128)S(1)}, f32[8,2,256]{2,0,1:T(8,128)S(1)}, u32[]{:S(2)}, u32[]{:S(2)}) collective-permute-start(f32[8,2,256]{2,0,1:T(8,128)S(1)} %dynamic-slice_bitcast_fusion), channel_id=1, source_target_pairs={{0,1},{1,0},{2,3},{3,2},{4,5},{5,4},{6,7},{7,6},{8,9},{9,8},{10,11... | collective-permute-start | bytes 49160 | tf_op jit(solution)/shard_map/ppermute | solution.py:258

commit v3 on v2

v3 whole, which is shorter than its diff:
```python
import jax
import jax.numpy as jnp
from jax import lax
from jax.experimental import pallas as pl
from jax.experimental.pallas import tpu as pltpu
from jax.sharding import PartitionSpec as P

MESH = pl.DeviceIdType.MESH
def place():
    gx, gy = lax.axis_index("gx"), lax.axis_index("gy")
    return gx // 4, gx // 2 % 2, gx % 2, gy // 4, gy % 4


def device(x, zh, core, zl, y):
    return (x * 4 + zh * 2 + core, zl * 4 + y)


def greet(peers):
    barrier = pltpu.get_barrier_semaphore()
    for peer in peers:
        pl.semaphore_signal(barrier, inc=1, device_id=peer, device_id_type=MESH)
    pl.semaphore_wait(barrier, len(peers))


def source_offset(turn):
    return jnp.where(turn % 2 == 1, (turn + 1) // 2, (16 - turn // 2) % 16)


LAG = 4


def far_field_kernel(
    partial, offsets, operators, out,
    mine, arrived, held, other, ops, planes, total, part, from_y, summed, rounded, from_z,
    ops_sem, pair_send, pair_recv, z_send, z_recv, y_send, y_recv, x_send, x_recv, c_send, c_recv,
    sy_send, sy_recv, sz_send, sz_recv,
):
    x, zh, core, zl, y = place()
    zp = zh * 8 + zl
    parity = y % 2
    y_of = [(y + d) % 4 for d in (1, 2, 3)]
    x_peers = [device((x + d) % 4, zh, core, zl, y) for d in (1, 3)]
    y_peers = [device(x, zh, core, zl, to) for to in y_of]
    pair = device(x, zh, core, zl, y + 1 - 2 * parity)
    partner = device(x, zh, 1 - core, zl, y)

    def z_peer(offset):
        position = (zp + offset) % 16
        return device(x, position // 8, core, position % 8, y)

    def remote(src, dst, send, recv, target):
        return pltpu.make_async_remote_copy(
            src_ref=src, dst_ref=dst, send_sem=send, recv_sem=recv, device_id=target, device_id_type=MESH
        )

    def along_z(offset):
        to = (zp + offset) % 16
        return remote(mine, held.at[1 + core + zh - to // 8, zl, y], z_send.at[offset], z_recv.at[offset], z_peer(offset))

    def spot_of(turn):
        position = (zp + 16 - source_offset(turn)) % 16
        return position, 1 + core + position // 8 - zh, position % 8

    def along_y(turn, d):
        position, plane, row = spot_of(turn)
        piece = held.at[plane, row, y]
        return remote(piece, piece, y_send.at[position, d], y_recv.at[position, d], y_peers[d])

    def along_x(turn):
        position, plane, row = spot_of(turn)
        to = (x + jnp.where(plane >= 2, 1, 3)) % 4
        return remote(
            held.at[plane, row], held.at[(plane + 2) % 4, row], x_send.at[position], x_recv.at[position],
            device(to, zh, core, zl, y),
        )

    def across(turn, far):
        position, plane, row = spot_of(turn)
        plane = (plane + 2 * far) % 4
        return remote(held.at[plane, row], other.at[plane, row], c_send.at[position, far], c_recv.at[position, far], partner)

    fetch = pltpu.make_async_copy(operators, ops, ops_sem)
    fetch.start()
    greet([z_peer(d) for d in range(1, 16)] + y_peers + x_peers + [partner])

    swap = remote(partial.at[1 - parity], arrived, pair_send, pair_recv, pair)
    swap.start()
    swap.wait()
    coarse = (partial[parity] + arrived[...]).astype(jnp.bfloat16)
    mine[...] = coarse
    held[1 + core, zl, y] = coarse

    def send_z(turn, carry):
        along_z((16 - source_offset(turn)) % 16).start()
        return carry

    lax.fori_loop(1, 16, send_z, 0)

    def turns(turn, carry):
        @pl.when(turn < 16)
        def _():
            @pl.when(turn > 0)
            def _():
                along_z(source_offset(turn)).wait_recv()

            for d in range(3):
                along_y(turn, d).start()

        @pl.when((turn >= LAG) & (turn < 16 + LAG))
        def _():
            for d in range(3):
                along_y(turn - LAG, d).wait_recv()
            along_x(turn - LAG).start()
            across(turn - LAG, 0).start()

        @pl.when(turn >= 2 * LAG)
        def _():
            along_x(turn - 2 * LAG).wait_recv()
            across(turn - 2 * LAG, 1).start()

        return carry

    lax.fori_loop(0, 16 + 2 * LAG, turns, 0)

    def drain(turn, carry):
        @pl.when(turn > 0)
        def _():
            along_z(turn).wait_send()

        for d in range(3):
            along_y(turn, d).wait_send()
        along_x(turn).wait_send()
        across(turn, 0).wait()
        across(turn, 1).wait()
        return carry

    lax.fori_loop(0, 16, drain, 0)

    def widen(row, carry):
        for shift in range(-3, 4):
            for half in range(2):
                source = other if shift % 2 else held
                index = (shift + 3) // 2 if shift % 2 else (shift + 2) // 2 + core
                wide = source[index, row, 2 * half : 2 * half + 2].reshape(32, 256).astype(jnp.float32)
                for lanes in range(2):
                    piece = wide[:, lanes * 128 : lanes * 128 + 128]
                    planes[lanes, shift + 3, 2 * row + half, 0:32] = piece
                    planes[lanes, shift + 3, 2 * row + half, 32:64] = piece
        return carry

    lax.fori_loop(0, 8, widen, 0)
    total[...] = jnp.zeros_like(total)
    fetch.wait()

    def one(entry, carry):
        dx, dy, dz = offsets[entry * 3] + 3, offsets[entry * 3 + 1], offsets[entry * 3 + 2]
        start = 2 * ((dz + 16) % 16)
        halves = [
            jnp.concatenate([planes[lanes, dx, (line + dy + 16) % 16, pl.ds(start, 32), :] for line in range(16)], axis=0)
            for lanes in range(2)
        ]
        rolled = jnp.concatenate(halves, axis=1).astype(jnp.bfloat16)
        total[...] += jnp.dot(rolled, ops[entry], preferred_element_type=jnp.float32)
        return carry

    lax.fori_loop(0, 16, one, 0)
    part[...] = total[...].astype(jnp.bfloat16).reshape(8, 4, 16, 256)

    sums_y = [remote(part.at[:, y_of[d]], from_y.at[d], sy_send.at[d], sy_recv.at[d], y_peers[d]) for d in range(3)]
    for copy in sums_y:
        copy.start()
    for copy in sums_y:
        copy.wait()
    line = part[:, y].astype(jnp.float32)
    for d in range(3):
        line = line + from_y[d].astype(jnp.float32)
    summed[...] = line
    rounded[...] = line.astype(jnp.bfloat16)
    z_of = [(zl + d) % 8 for d in range(1, 8)]
    sums_z = [
        remote(rounded.at[z_of[d]], from_z.at[d], sz_send.at[d], sz_recv.at[d], device(x, zh, core, z_of[d], y))
        for d in range(7)
    ]
    for copy in sums_z:
        copy.start()
    for copy in sums_z:
        copy.wait()
    result = summed[zl]
    for d in range(7):
        result = result + from_z[d].astype(jnp.float32)
    out[...] = result


def far_field(partial, offsets, operators):
    dma, half = pltpu.SemaphoreType.DMA, jnp.bfloat16
    return pl.pallas_call(
        far_field_kernel,
        out_shape=jax.ShapeDtypeStruct((16, 256), jnp.float32),
        in_specs=[
            pl.BlockSpec(memory_space=pltpu.VMEM),
            pl.BlockSpec(memory_space=pltpu.SMEM),
            pl.BlockSpec(memory_space=pl.ANY),
        ],
        out_specs=pl.BlockSpec(memory_space=pltpu.VMEM),
        scratch_shapes=[
            pltpu.VMEM((16, 256), half),
            pltpu.VMEM((16, 256), jnp.float32),
            pltpu.VMEM((4, 8, 4, 16, 256), half),
            pltpu.VMEM((4, 8, 4, 16, 256), half),
            pltpu.VMEM((16, 256, 256), half),
            pltpu.VMEM((2, 7, 16, 64, 128), jnp.float32),
            pltpu.VMEM((512, 256), jnp.float32),
            pltpu.VMEM((8, 4, 16, 256), half),
            pltpu.VMEM((3, 8, 16, 256), half),
            pltpu.VMEM((8, 16, 256), jnp.float32),
            pltpu.VMEM((8, 16, 256), half),
            pltpu.VMEM((7, 16, 256), half),
            dma, dma, dma,
            dma((16,)), dma((16,)),
            dma((16, 3)), dma((16, 3)),
            dma((16,)), dma((16,)),
            dma((16, 2)), dma((16, 2)),
            dma((3,)), dma((3,)), dma((7,)), dma((7,)),
        ],
        compiler_params=pltpu.CompilerParams(collective_id=0, has_side_effects=True),
        name="far_field",
    )(partial, offsets, operators)


def on_device(fine_multipoles, m2m_ops, m2l_ops, offsets):
    parity = lax.axis_index("gy") % 2
    selected = lax.dynamic_index_in_dim(m2m_ops, parity, 1, keepdims=False)
    children = fine_multipoles[:, 0].reshape(2, 16, 2, 2, 256)
    partial = jnp.einsum("azcri,acio->zro", children, selected, preferred_element_type=jnp.float32)
    result = far_field(partial.reshape(2, 16, 256), offsets.reshape(-1), m2l_ops)
    return result.reshape(1, 8, 2, 256)


def solution(mesh):
    return jax.shard_map(
        on_device,
        mesh=mesh,
        in_specs=(P("gx", "gy", None, None, None), P(), P("gy", None, None), P("gy", None)),
        out_specs=P("gx", "gy", None, None),
        check_vma=False,
    )
```

time: 77.5 us -> 66 us (0.85)
  Pallas kernels: 67.5 us -> 60 us
  starting transfers between devices: 4.02 us -> 0 us
    pallas_call x3 -> x1, Pallas kernels: 67.5 us -> 60 us  [far_field(): pl.pallas_call(far_field_kernel, out_shape=jax.ShapeDtypeStruct((16, 256)...]
    ppermute x1 -> x0, starting transfers between devices: 4.02 us -> none  [on_device(): arrived = lax.ppermute(sent, 'gy', [(i, i ^ 1) for i in range(32)])]
  transfers between devices with their start and end apart: 1 -> 0, of which waited for: 0 -> 0; matrix products, arithmetic and copies ran while one was open for 2% -> 0% of each run, Pallas kernels for 0% -> 0%
where the time goes in v3:
time: 66 us; the launch traced here: 65.7 us
  Pallas kernels  60 us (91%)
  local copies, waits for them, and re-layouts  4.59 us (7%)
  matrix products  1.03 us (2%)
    pallas_call x1, Pallas kernels, far_field(): pl.pallas_call(far_field_kernel, out_shape=jax.ShapeDtypeStruct((16, 256)...  60 us
    unnamed x3, local copies, waits for them, and re-layouts  1.98 us
    reshape x1, local copies, waits for them, and re-layouts, on_device(): return result.reshape(1, 8, 2, 256)  1.34 us

profile of v3, /device:TPU:1, one launch (start us, length us, event | category | flops | bytes accessed | tf_op | source)
XLA Modules:
  0.0 65.7 jit_solution(8165739526872284222)
XLA Ops:
  0.0 0.0 copy-start
  0.0 1.2 %copy-done = bf16[2,2,2,256,256]{4,3,2,1,0:T(8,128)(2,1)S(1)} copy-done((bf16[2,2,2,256,256]{4,3,2,1,0:T(8,128)(2,1)S(1)}, bf16[2,2,2,256,256]{4,3,2,1,0:T(8,128)(2,1)}, u32[]{:S(2)}) %copy-start) | copy-done | bytes 1048600
  1.2 1.0 %convolution_bitcast_fusion = f32[16,2,256]{2,0,1:T(8,128)S(1)} fusion(bf16[2,2,2,256,256]{4,3,2,1,0:T(8,128)(2,1)S(1)} %copy-done, s32[]{:T(128)S(6)} %select_n.12, bf16[2,16,2,2,256]{4,3,2,1,0:T(2,128)(2,1)} %bitcast.13), kind=kOutput, calls=%fused_computation | convolution fusion | flops 16777216 | bytes 622596 | tf_op jit(solution)/shard_map/azcri,acio->zro/dot_general | solution.py:234
  2.3 0.6 reshape.9.partial
  2.9 0.8 %copy.10 = s32[16,3]{1,0:T(8,128)S(1)} copy(s32[16,3]{0,1:T(4,128)} %param.7) | data formatting | bytes 384 | tf_op args[3]
  3.7 0.6 reshape.10.offsets
  4.3 60.0 %far_field.1 = f32[16,256]{1,0:T(8,128)} custom-call(f32[2,16,256]{2,1,0:T(8,128)} %reshape.9.partial, s32[48]{0:T(128)} %reshape.10.offsets, bf16[16,256,256]{2,1,0:T(8,128)(2,1)} %operators.1), custom_call_target="tpu_custom_call" | custom-call | tf_op jit(solution)/shard_map/far_field/pallas_call | solution.py:196
  64.3 1.3 %reshape.11 = f32[1,8,2,256]{3,2,1,0:T(2,128)} reshape(f32[16,256]{1,0:T(8,128)} %far_field.1) | data formatting | bytes 32768 | tf_op jit(solution)/shard_map/reshape | solution.py:236
  (1 shorter events, 0.0 us)
Async XLA Ops:
  0.0 1.2 %copy-start = (bf16[2,2,2,256,256]{4,3,2,1,0:T(8,128)(2,1)S(1)}, bf16[2,2,2,256,256]{4,3,2,1,0:T(8,128)(2,1)}, u32[]{:S(2)}) copy-start(bf16[2,2,2,256,256]{4,3,2,1,0:T(8,128)(2,1)} %param.5) | copy-start | bytes 3145732

commit v4 on v3

--- a/solution.py
+++ b/solution.py
@@ -19,7 +19,12 @@
     barrier = pltpu.get_barrier_semaphore()
     for peer in peers:
         pl.semaphore_signal(barrier, inc=1, device_id=peer, device_id_type=MESH)
-    pl.semaphore_wait(barrier, len(peers))
+
+
+def child_rows(child):
+    to = lax.broadcasted_iota(jnp.int32, (32, 64), 0)
+    source = lax.broadcasted_iota(jnp.int32, (32, 64), 1)
+    return jnp.where(source == to // 2 * 4 + child * 2 + to % 2, 1.0, 0.0).astype(jnp.bfloat16)
 
 
 def source_offset(turn):
@@ -30,9 +35,9 @@
 
 
 def far_field_kernel(
-    partial, offsets, operators, out,
-    mine, arrived, held, other, ops, planes, total, part, from_y, summed, rounded, from_z,
-    ops_sem, pair_send, pair_recv, z_send, z_recv, y_send, y_recv, x_send, x_recv, c_send, c_recv,
+    fine, upward, offsets, operators, out,
+    up, partial, mine, arrived, held, other, ops, planes, total, part, from_y, summed, rounded, from_z,
+    ops_sem, up_sem, pair_send, pair_recv, z_send, z_recv, y_send, y_recv, x_send, x_recv, c_send, c_recv,
     sy_send, sy_recv, sz_send, sz_recv,
 ):
     x, zh, core, zl, y = place()
@@ -79,9 +84,21 @@
         plane = (plane + 2 * far) % 4
         return remote(held.at[plane, row], other.at[plane, row], c_send.at[position, far], c_recv.at[position, far], partner)
 
+    peers = [z_peer(d) for d in range(1, 16)] + y_peers + x_peers + [partner]
+    greet(peers)
+    lift = pltpu.make_async_copy(upward.at[:, parity], up, up_sem)
+    lift.start()
     fetch = pltpu.make_async_copy(operators, ops, ops_sem)
     fetch.start()
-    greet([z_peer(d) for d in range(1, 16)] + y_peers + x_peers + [partner])
+    picked = [
+        jnp.dot(child_rows(c), fine[a, 0].reshape(64, 256), preferred_element_type=jnp.float32).astype(jnp.bfloat16)
+        for a in range(2)
+        for c in range(2)
+    ]
+    lift.wait()
+    terms = [jnp.dot(picked[n], up[n // 2, n % 2], preferred_element_type=jnp.float32) for n in range(4)]
+    partial[...] = ((terms[0] + terms[1]) + (terms[2] + terms[3])).reshape(2, 16, 256)
+    pl.semaphore_wait(pltpu.get_barrier_semaphore(), len(peers))
 
     swap = remote(partial.at[1 - parity], arrived, pair_send, pair_recv, pair)
     swap.start()
@@ -153,7 +170,7 @@
     fetch.wait()
 
     def one(entry, carry):
-        dx, dy, dz = offsets[entry * 3] + 3, offsets[entry * 3 + 1], offsets[entry * 3 + 2]
+        dx, dy, dz = offsets[0, entry] + 3, offsets[1, entry], offsets[2, entry]
         start = 2 * ((dz + 16) % 16)
         halves = [
             jnp.concatenate([planes[lanes, dx, (line + dy + 16) % 16, pl.ds(start, 32), :] for line in range(16)], axis=0)
@@ -188,21 +205,24 @@
     result = summed[zl]
     for d in range(7):
         result = result + from_z[d].astype(jnp.float32)
-    out[...] = result
-
-
-def far_field(partial, offsets, operators):
+    out[...] = result.reshape(1, 8, 2, 256)
+
+
+def far_field(fine, upward, offsets, operators):
     dma, half = pltpu.SemaphoreType.DMA, jnp.bfloat16
     return pl.pallas_call(
         far_field_kernel,
-        out_shape=jax.ShapeDtypeStruct((16, 256), jnp.float32),
+        out_shape=jax.ShapeDtypeStruct((1, 8, 2, 256), jnp.float32),
         in_specs=[
             pl.BlockSpec(memory_space=pltpu.VMEM),
+            pl.BlockSpec(memory_space=pl.ANY),
             pl.BlockSpec(memory_space=pltpu.SMEM),
             pl.BlockSpec(memory_space=pl.ANY),
         ],
         out_specs=pl.BlockSpec(memory_space=pltpu.VMEM),
         scratch_shapes=[
+            pltpu.VMEM((2, 2, 256, 256), half),
+            pltpu.VMEM((2, 16, 256), jnp.float32),
             pltpu.VMEM((16, 256), half),
             pltpu.VMEM((16, 256), jnp.float32),
             pltpu.VMEM((4, 8, 4, 16, 256), half),
@@ -215,7 +235,7 @@
             pltpu.VMEM((8, 16, 256), jnp.float32),
             pltpu.VMEM((8, 16, 256), half),
             pltpu.VMEM((7, 16, 256), half),
-            dma, dma, dma,
+            dma, dma, dma, dma,
             dma((16,)), dma((16,)),
             dma((16, 3)), dma((16, 3)),
             dma((16,)), dma((16,)),
@@ -224,16 +244,11 @@
         ],
         compiler_params=pltpu.CompilerParams(collective_id=0, has_side_effects=True),
         name="far_field",
-    )(partial, offsets, operators)
+    )(fine, upward, offsets, operators)
 
 
 def on_device(fine_multipoles, m2m_ops, m2l_ops, offsets):
-    parity = lax.axis_index("gy") % 2
-    selected = lax.dynamic_index_in_dim(m2m_ops, parity, 1, keepdims=False)
-    children = fine_multipoles[:, 0].reshape(2, 16, 2, 2, 256)
-    partial = jnp.einsum("azcri,acio->zro", children, selected, preferred_element_type=jnp.float32)
-    result = far_field(partial.reshape(2, 16, 256), offsets.reshape(-1), m2l_ops)
-    return result.reshape(1, 8, 2, 256)
+    return far_field(fine_multipoles, m2m_ops, offsets.T, m2l_ops)
 
 
 def solution(mesh):

time: 66 us -> 61.5 us (0.932)
  local copies, waits for them, and re-layouts: 4.59 us -> 1.32 us
  matrix products: 1.03 us -> 0 us
    reshape x3 -> x0, local copies, waits for them, and re-layouts: 2.58 us -> none  [the longest x1 1.34 us: on_device(): return result.reshape(1, 8, 2, 256)]
    dot_general x1 -> x0, matrix products: 1.03 us -> none  [on_device(): jnp.einsum('azcri,acio->zro', children, selected, preferred_element_type=...]
    unnamed x3 -> x1, local copies, waits for them, and re-layouts: 1.98 us -> 1.32 us
where the time goes in v4:
time: 61.5 us; the launch traced here: 61.3 us
  Pallas kernels  60 us (98%)
  local copies, waits for them, and re-layouts  1.32 us (2%)
    pallas_call x1, Pallas kernels, far_field(): pl.pallas_call(far_field_kernel, out_shape=jax.ShapeDtypeStruct((1, 8, 2,...  60 us
    unnamed x1, local copies, waits for them, and re-layouts  1.32 us

profile of v4, /device:TPU:1, one launch (start us, length us, event | category | flops | bytes accessed | tf_op | source)
XLA Modules:
  0.0 61.3 jit_solution(11829270628029447459)
XLA Ops:
  0.0 60.0 %far_field.1 = f32[1,8,2,256]{3,2,1,0:T(2,128)} custom-call(bf16[2,1,32,2,256]{4,3,2,1,0:T(2,128)(2,1)} %fine.1, bf16[2,2,2,256,256]{4,3,2,1,0:T(8,128)(2,1)} %upward.1, s32[3,16]{1,0:T(4,128)} %bitcast.1, bf16[16,256,256]{2,1,0:T(8,128)(2,1)} %operators.1), custom_call_target="tpu_custom_call" | custom-call | tf_op jit(solution)/shard_map/far_field/pallas_call | solution.py:213
  60.0 1.3 %copy.6 = f32[1,8,2,256]{3,2,1,0:T(2,128)} copy(f32[1,8,2,256]{3,2,1,0:T(2,128)} %far_field.1) | data formatting | bytes 32768

commit v5 on v4

--- a/solution.py
+++ b/solution.py
@@ -31,7 +31,7 @@
     return jnp.where(turn % 2 == 1, (turn + 1) // 2, (16 - turn // 2) % 16)
 
 
-LAG = 4
+Y_LAG, X_LAG = 12, 8
 
 
 def far_field_kernel(
@@ -123,21 +123,21 @@
             for d in range(3):
                 along_y(turn, d).start()
 
-        @pl.when((turn >= LAG) & (turn < 16 + LAG))
+        @pl.when((turn >= Y_LAG) & (turn < 16 + Y_LAG))
         def _():
             for d in range(3):
-                along_y(turn - LAG, d).wait_recv()
-            along_x(turn - LAG).start()
-            across(turn - LAG, 0).start()
-
-        @pl.when(turn >= 2 * LAG)
-        def _():
-            along_x(turn - 2 * LAG).wait_recv()
-            across(turn - 2 * LAG, 1).start()
-
-        return carry
-
-    lax.fori_loop(0, 16 + 2 * LAG, turns, 0)
+                along_y(turn - Y_LAG, d).wait_recv()
+            along_x(turn - Y_LAG).start()
+            across(turn - Y_LAG, 0).start()
+
+        @pl.when(turn >= Y_LAG + X_LAG)
+        def _():
+            along_x(turn - Y_LAG - X_LAG).wait_recv()
+            across(turn - Y_LAG - X_LAG, 1).start()
+
+        return carry
+
+    lax.fori_loop(0, 16 + Y_LAG + X_LAG, turns, 0)
 
     def drain(turn, carry):
         @pl.when(turn > 0)
@@ -166,26 +166,40 @@
         return carry
 
     lax.fori_loop(0, 8, widen, 0)
-    total[...] = jnp.zeros_like(total)
     fetch.wait()
 
-    def one(entry, carry):
-        dx, dy, dz = offsets[0, entry] + 3, offsets[1, entry], offsets[2, entry]
-        start = 2 * ((dz + 16) % 16)
-        halves = [
-            jnp.concatenate([planes[lanes, dx, (line + dy + 16) % 16, pl.ds(start, 32), :] for line in range(16)], axis=0)
-            for lanes in range(2)
-        ]
-        rolled = jnp.concatenate(halves, axis=1).astype(jnp.bfloat16)
-        total[...] += jnp.dot(rolled, ops[entry], preferred_element_type=jnp.float32)
-        return carry
-
-    lax.fori_loop(0, 16, one, 0)
-    part[...] = total[...].astype(jnp.bfloat16).reshape(8, 4, 16, 256)
-
-    sums_y = [remote(part.at[:, y_of[d]], from_y.at[d], sy_send.at[d], sy_recv.at[d], y_peers[d]) for d in range(3)]
-    for copy in sums_y:
-        copy.start()
+    def half_sums(odd):
+        total[...] = jnp.zeros_like(total)
+
+        def one(entry, carry):
+            dx, dy, dz = offsets[0, entry] + 3, offsets[1, entry], offsets[2, entry]
+            start = 2 * ((dz + 16) % 16)
+            halves = [
+                jnp.concatenate(
+                    [planes[lanes, dx, (2 * row + odd + dy + 16) % 16, pl.ds(start, 32), :] for row in range(8)], axis=0
+                )
+                for lanes in range(2)
+            ]
+            rolled = jnp.concatenate(halves, axis=1).astype(jnp.bfloat16)
+            total[...] += jnp.dot(rolled, ops[entry], preferred_element_type=jnp.float32)
+            return carry
+
+        lax.fori_loop(0, 16, one, 0)
+        part[:, pl.ds(2 * odd, 2)] = total[...].astype(jnp.bfloat16).reshape(8, 2, 16, 256)
+
+    def sum_to(to):
+        slot = (to + 3 - y) % 4
+        return remote(
+            part.at[:, to], from_y.at[slot], sy_send.at[slot], sy_recv.at[slot], device(x, zh, core, zl, to)
+        )
+
+    first = 1 - y // 2
+    half_sums(first)
+    sum_to(2 * first).start()
+    sum_to(2 * first + 1).start()
+    half_sums(1 - first)
+    sum_to(y + 1 - 2 * parity).start()
+    sums_y = [sum_to(to) for to in y_of]
     for copy in sums_y:
         copy.wait()
     line = part[:, y].astype(jnp.float32)
@@ -229,7 +243,7 @@
             pltpu.VMEM((4, 8, 4, 16, 256), half),
             pltpu.VMEM((16, 256, 256), half),
             pltpu.VMEM((2, 7, 16, 64, 128), jnp.float32),
-            pltpu.VMEM((512, 256), jnp.float32),
+            pltpu.VMEM((256, 256), jnp.float32),
             pltpu.VMEM((8, 4, 16, 256), half),
             pltpu.VMEM((3, 8, 16, 256), half),
             pltpu.VMEM((8, 16, 256), jnp.float32),

time: 61.5 us -> 59 us (0.959)
  Pallas kernels: 60 us -> 57 us
    pallas_call x1, Pallas kernels: 60 us -> 57 us  [far_field(): pl.pallas_call(far_field_kernel, out_shape=jax.ShapeDtypeStruct((1, 8, 2,...]
where the time goes in v5:
time: 59 us; the launch traced here: 58.4 us
  Pallas kernels  57 us (97%)
  local copies, waits for them, and re-layouts  1.32 us (2%)
    pallas_call x1, Pallas kernels, far_field(): pl.pallas_call(far_field_kernel, out_shape=jax.ShapeDtypeStruct((1, 8, 2,...  57 us
    unnamed x1, local copies, waits for them, and re-layouts  1.32 us

profile of v5, /device:TPU:1, one launch (start us, length us, event | category | flops | bytes accessed | tf_op | source)
XLA Modules:
  0.0 58.4 jit_solution(6400817943265958832)
XLA Ops:
  0.0 57.0 %far_field.1 = f32[1,8,2,256]{3,2,1,0:T(2,128)} custom-call(bf16[2,1,32,2,256]{4,3,2,1,0:T(2,128)(2,1)} %fine.1, bf16[2,2,2,256,256]{4,3,2,1,0:T(8,128)(2,1)} %upward.1, s32[3,16]{1,0:T(4,128)} %bitcast.1, bf16[16,256,256]{2,1,0:T(8,128)(2,1)} %operators.1), custom_call_target="tpu_custom_call" | custom-call | tf_op jit(solution)/shard_map/far_field/pallas_call | solution.py:227
  57.1 1.3 %copy.6 = f32[1,8,2,256]{3,2,1,0:T(2,128)} copy(f32[1,8,2,256]{3,2,1,0:T(2,128)} %far_field.1) | data formatting | bytes 32768

commit v6 on v5

--- a/solution.py
+++ b/solution.py
@@ -31,7 +31,7 @@
     return jnp.where(turn % 2 == 1, (turn + 1) // 2, (16 - turn // 2) % 16)
 
 
-Y_LAG, X_LAG = 12, 8
+Y_LAG, X_LAG = 9, 12
 
 
 def far_field_kernel(
@@ -139,6 +139,23 @@
 
     lax.fori_loop(0, 16 + Y_LAG + X_LAG, turns, 0)
 
+    def widen(shifts):
+        def one_row(row, carry):
+            for shift in shifts:
+                for half in range(2):
+                    source = other if shift % 2 else held
+                    index = (shift + 3) // 2 if shift % 2 else (shift + 2) // 2 + core
+                    wide = source[index, row, 2 * half : 2 * half + 2].reshape(32, 256).astype(jnp.float32)
+                    for lanes in range(2):
+                        piece = wide[:, lanes * 128 : lanes * 128 + 128]
+                        planes[lanes, shift + 3, 2 * row + half, 0:32] = piece
+                        planes[lanes, shift + 3, 2 * row + half, 32:64] = piece
+            return carry
+
+        lax.fori_loop(0, 8, one_row, 0)
+
+    widen((-2, 0, 2))
+
     def drain(turn, carry):
         @pl.when(turn > 0)
         def _():
@@ -153,19 +170,7 @@
 
     lax.fori_loop(0, 16, drain, 0)
 
-    def widen(row, carry):
-        for shift in range(-3, 4):
-            for half in range(2):
-                source = other if shift % 2 else held
-                index = (shift + 3) // 2 if shift % 2 else (shift + 2) // 2 + core
-                wide = source[index, row, 2 * half : 2 * half + 2].reshape(32, 256).astype(jnp.float32)
-                for lanes in range(2):
-                    piece = wide[:, lanes * 128 : lanes * 128 + 128]
-                    planes[lanes, shift + 3, 2 * row + half, 0:32] = piece
-                    planes[lanes, shift + 3, 2 * row + half, 32:64] = piece
-        return carry
-
-    lax.fori_loop(0, 8, widen, 0)
+    widen((-3, -1, 1, 3))
     fetch.wait()
 
     def half_sums(odd):

time: 59 us -> 58.8 us (level)
  no operation moved by 1% of the time
where the time goes in v6:
time: 58.8 us; the launch traced here: 58.1 us
  Pallas kernels  56.8 us (97%)
  local copies, waits for them, and re-layouts  1.32 us (2%)
    pallas_call x1, Pallas kernels, far_field(): pl.pallas_call(far_field_kernel, out_shape=jax.ShapeDtypeStruct((1, 8, 2,...  56.8 us
    unnamed x1, local copies, waits for them, and re-layouts  1.32 us

profile of v6, /device:TPU:1, one launch (start us, length us, event | category | flops | bytes accessed | tf_op | source)
XLA Modules:
  0.0 58.1 jit_solution(7195638236928220371)
XLA Ops:
  0.0 56.8 %far_field.1 = f32[1,8,2,256]{3,2,1,0:T(2,128)} custom-call(bf16[2,1,32,2,256]{4,3,2,1,0:T(2,128)(2,1)} %fine.1, bf16[2,2,2,256,256]{4,3,2,1,0:T(8,128)(2,1)} %upward.1, s32[3,16]{1,0:T(4,128)} %bitcast.1, bf16[16,256,256]{2,1,0:T(8,128)(2,1)} %operators.1), custom_call_target="tpu_custom_call" | custom-call | tf_op jit(solution)/shard_map/far_field/pallas_call | solution.py:232
  56.8 1.3 %copy.6 = f32[1,8,2,256]{3,2,1,0:T(2,128)} copy(f32[1,8,2,256]{3,2,1,0:T(2,128)} %far_field.1) | data formatting | bytes 32768

commit v7 on v6

--- a/solution.py
+++ b/solution.py
@@ -120,7 +120,7 @@
             def _():
                 along_z(source_offset(turn)).wait_recv()
 
-            for d in range(3):
+            for d in (1, 0, 2):
                 along_y(turn, d).start()
 
         @pl.when((turn >= Y_LAG) & (turn < 16 + Y_LAG))

time: 58.8 us -> 58.7 us (level)
  no operation moved by 1% of the time
where the time goes in v7:
time: 58.7 us; the launch traced here: 58.1 us
  Pallas kernels  56.7 us (97%)
  local copies, waits for them, and re-layouts  1.32 us (2%)
    pallas_call x1, Pallas kernels, far_field(): pl.pallas_call(far_field_kernel, out_shape=jax.ShapeDtypeStruct((1, 8, 2,...  56.7 us
    unnamed x1, local copies, waits for them, and re-layouts  1.32 us

profile of v7, /device:TPU:1, one launch (start us, length us, event | category | flops | bytes accessed | tf_op | source)
XLA Modules:
  0.0 58.1 jit_solution(9587951867418206398)
XLA Ops:
  0.0 56.7 %far_field.1 = f32[1,8,2,256]{3,2,1,0:T(2,128)} custom-call(bf16[2,1,32,2,256]{4,3,2,1,0:T(2,128)(2,1)} %fine.1, bf16[2,2,2,256,256]{4,3,2,1,0:T(8,128)(2,1)} %upward.1, s32[3,16]{1,0:T(4,128)} %bitcast.1, bf16[16,256,256]{2,1,0:T(8,128)(2,1)} %operators.1), custom_call_target="tpu_custom_call" | custom-call | tf_op jit(solution)/shard_map/far_field/pallas_call | solution.py:232
  56.7 1.3 %copy.6 = f32[1,8,2,256]{3,2,1,0:T(2,128)} copy(f32[1,8,2,256]{3,2,1,0:T(2,128)} %far_field.1) | data formatting | bytes 32768
